TPU v7x, 256 devices: a whole 4x4x8 slice. The times are simulated.
256 devices in a mesh: replica: 8 (over x, core), outer: 4 (over y), link: 8 (over z).
Axes of the slice: x: 4, y: 4, z: 8, core: 2. Of those that a mesh axis runs over, the one named last changes fastest.
Arguments:
- link_in: bfloat16 [8, 16384, 256], P('replica', ('outer', 'link')), may hold values from -6 to 6
- path_in: bfloat16 [8, 4096, 256], P('replica', ('outer', 'link')), may hold values from -6 to 6
- hop_slots: int32 [8, 4096, 24], P('replica', ('outer', 'link')), may hold values from 0 to 2047
- hop_lens: int32 [8, 4096], P('replica', ('outer', 'link')), may hold values from 2 to 24
- failed: int32 [8, 16384], P('replica', ('outer', 'link')), may hold values 0 or 1
- serve_index: int32 [8, 32, 32, 64], P('replica', None, ('outer', 'link')), may hold values from 0 to 511
- link_grad: bfloat16 [8, 16384, 256], P('replica', ('outer', 'link')), may hold values from -6 to 6
- path_grad: bfloat16 [8, 4096, 256], P('replica', ('outer', 'link')), may hold values from -6 to 6
- gru_wx: bfloat16 [256, 768], replicated, may hold values from -0.375 to 0.375
- gru_wh: bfloat16 [256, 768], replicated, may hold values from -0.375 to 0.375
- gru_bias: float32 [768], replicated, may hold values from -3 to 3
- mlp_w1: bfloat16 [512, 256], replicated, may hold values from -0.25 to 0.25
- mlp_b1: float32 [256], replicated, may hold values from -3 to 3
- mlp_w2: bfloat16 [256, 256], replicated, may hold values from -0.375 to 0.375
- mlp_b2: float32 [256], replicated, may hold values from -3 to 3
Outputs:
- link_out: bfloat16 [8, 16384, 256], P('replica', ('outer', 'link'))
- path_out: bfloat16 [8, 4096, 256], P('replica', ('outer', 'link'))
- link_in_grad: float32 [8, 16384, 256], P('replica', ('outer', 'link'))
- path_in_grad: float32 [8, 4096, 256], P('replica', ('outer', 'link'))
- grad_wx: float32 [256, 768], replicated
- grad_wh: float32 [256, 768], replicated
- grad_bias: float32 [768], replicated
- grad_w1: float32 [512, 256], replicated
- grad_b1: float32 [256], replicated
- grad_w2: float32 [256, 256], replicated
- grad_b2: float32 [256], replicated
Inputs may be any that keep to these rules, and one draw needn't show every extreme that they name: `serve_index`: entry [s, d, o, c] names, among the 512 links of owner device o, the link in request slot c of device d; a link may fill several slots. `hop_slots`: slot o * 64 + c is request slot c of the flow's own device towards owner o; entries at hops past the flow's length are ignored. 1 marks a failed link.
All inputs are finite; a program needn't handle non-finite values. No bound on the sum of `failed` on one device may be relied on, other than what follows from the above.
Results may differ from a plain program's by a relative error of at most 0.0067.
Values may be sent and summed in bfloat16 or wider, within the bound.
No kernel may reach another device: no remote copies, remote signals or barrier semaphores. Data moves between devices by JAX's collectives and lax.ppermute only.
A program may use at most 128 MiB of HBM per device.

v0:
```python
import jax
import jax.numpy as jnp
from jax import lax
from jax.sharding import PartitionSpec as P


def gate_terms(state_now, hop_input, input_weight, hidden_weight, gate_bias):
    from_input = jnp.dot(hop_input, input_weight, preferred_element_type=jnp.float32) + gate_bias
    from_state = jnp.dot(
        state_now.astype(jnp.bfloat16), hidden_weight, preferred_element_type=jnp.float32
    )
    return (from_input, from_state)


def gru_cell(state_now, from_input, from_state):
    feat_width = state_now.shape[1]
    update = jax.nn.sigmoid(from_input[:, :feat_width] + from_state[:, :feat_width])
    reset = jax.nn.sigmoid(
        from_input[:, feat_width : 2 * feat_width] + from_state[:, feat_width : 2 * feat_width]
    )
    candidate = jnp.tanh(from_input[:, 2 * feat_width :] + reset * from_state[:, 2 * feat_width :])
    return (candidate + update * (state_now - candidate), update, reset, candidate)


def gru_forward(path_start, hop_inputs, live_mask, input_weight, hidden_weight, gate_bias):

    def advance(state_now, scan_item):
        hop_input, live_now = scan_item
        from_input, from_state = gate_terms(
            state_now, hop_input, input_weight, hidden_weight, gate_bias
        )
        stepped = gru_cell(state_now, from_input, from_state)[0]
        state_next = jnp.where(live_now[:, None] > 0, stepped, state_now)
        return (state_next, (state_next,))

    return lax.scan(advance, path_start.astype(jnp.float32), (hop_inputs, live_mask))[1]


def back_step(
    carried, hop_input, state_now, live_now, hop_grad, from_input, from_state, input_tr, hidden_tr
):
    grad_state, grad_wx, grad_wh, grad_bias = carried
    feat_width = state_now.shape[1]
    live_col = live_now[:, None]
    grad_state = grad_state + live_col * hop_grad
    update, reset, candidate = gru_cell(state_now, from_input, from_state)[1:]
    pre_update = grad_state * (state_now - candidate) * update * (1.0 - update)
    pre_cand = grad_state * (1.0 - update) * (1.0 - candidate * candidate)
    pre_reset = pre_cand * from_state[:, 2 * feat_width :] * reset * (1.0 - reset)
    grad_in = jnp.concatenate([pre_update, pre_reset, pre_cand], axis=1) * live_col
    grad_hid = jnp.concatenate([pre_update, pre_reset, pre_cand * reset], axis=1) * live_col
    in_bf = grad_in.astype(jnp.bfloat16)
    hid_bf = grad_hid.astype(jnp.bfloat16)
    grad_prev = jnp.where(
        live_col > 0,
        grad_state * update + jnp.dot(hid_bf, hidden_tr, preferred_element_type=jnp.float32),
        grad_state,
    )
    grad_input = jnp.dot(in_bf, input_tr, preferred_element_type=jnp.float32)
    grad_wx = grad_wx + jnp.dot(hop_input.T, in_bf, preferred_element_type=jnp.float32)
    grad_wh = grad_wh + jnp.dot(
        state_now.astype(jnp.bfloat16).T, hid_bf, preferred_element_type=jnp.float32
    )
    grad_bias = grad_bias + jnp.sum(grad_in, axis=0)
    return ((grad_prev, grad_wx, grad_wh, grad_bias), grad_input)


def gru_backward(
    path_start,
    states,
    hop_inputs,
    live_mask,
    hop_grads,
    path_grad,
    input_weight,
    hidden_weight,
    gate_bias,
):
    feat_width = path_start.shape[1]
    prior_states = jnp.concatenate([path_start.astype(jnp.float32)[None], states[:-1]], axis=0)
    input_tr = input_weight.T
    hidden_tr = hidden_weight.T
    initial = (
        path_grad.astype(jnp.float32),
        jnp.zeros((feat_width, 3 * feat_width), jnp.float32),
        jnp.zeros((feat_width, 3 * feat_width), jnp.float32),
        jnp.zeros((3 * feat_width,), jnp.float32),
    )

    def retreat(carried, scan_item):
        hop_input, state_now, live_now, hop_grad = scan_item
        from_input, from_state = gate_terms(
            state_now, hop_input, input_weight, hidden_weight, gate_bias
        )
        return back_step(
            carried,
            hop_input,
            state_now,
            live_now,
            hop_grad,
            from_input,
            from_state,
            input_tr,
            hidden_tr,
        )

    scan_items = (hop_inputs, prior_states, live_mask, hop_grads)
    return lax.scan(retreat, initial, scan_items, reverse=True)


def link_forward(link_rows, agg_bf, keep_col, mlp_w1, mlp_b1, mlp_w2, mlp_b2):
    feat_width = link_rows.shape[1]
    pre_act = (
        jnp.dot(link_rows, mlp_w1[:feat_width], preferred_element_type=jnp.float32)
        + jnp.dot(agg_bf, mlp_w1[feat_width:], preferred_element_type=jnp.float32)
        + mlp_b1
    )
    activ = jax.nn.silu(pre_act).astype(jnp.bfloat16)
    value = (
        link_rows.astype(jnp.float32)
        + jnp.dot(activ, mlp_w2, preferred_element_type=jnp.float32)
        + mlp_b2
    )
    return ((keep_col * value).astype(jnp.bfloat16), pre_act, activ)


def link_backward(link_grad_rows, link_rows, agg_bf, keep_col, pre_act, activ, mlp_w1, mlp_w2):
    feat_width = link_rows.shape[1]
    grad_val = keep_col * link_grad_rows.astype(jnp.float32)
    val_bf = grad_val.astype(jnp.bfloat16)
    grad_w2 = jnp.dot(activ.T, val_bf, preferred_element_type=jnp.float32)
    grad_b2 = jnp.sum(grad_val, axis=0)
    grad_act = jnp.dot(val_bf, mlp_w2.T, preferred_element_type=jnp.float32)
    sigma = jax.nn.sigmoid(pre_act)
    grad_pre = grad_act * sigma * (1.0 + pre_act * (1.0 - sigma))
    pre_bf = grad_pre.astype(jnp.bfloat16)
    grad_w1 = jnp.concatenate(
        [
            jnp.dot(link_rows.T, pre_bf, preferred_element_type=jnp.float32),
            jnp.dot(agg_bf.T, pre_bf, preferred_element_type=jnp.float32),
        ],
        axis=0,
    )
    grad_b1 = jnp.sum(grad_pre, axis=0)
    link_direct = grad_val + jnp.dot(
        pre_bf, mlp_w1[:feat_width].T, preferred_element_type=jnp.float32
    )
    agg_grad = jnp.dot(pre_bf, mlp_w1[feat_width:].T, preferred_element_type=jnp.float32).astype(
        jnp.bfloat16
    )
    return (link_direct, agg_grad, (grad_w1, grad_b1, grad_w2, grad_b2))


def swap_slots(blocks):
    return lax.all_to_all(blocks, ("outer", "link"), split_axis=0, concat_axis=0, tiled=True)


def body(
    link_in,
    path_in,
    hop_slots,
    hop_lens,
    failed,
    serve_index,
    link_grad,
    path_grad,
    gru_wx,
    gru_wh,
    gru_bias,
    mlp_w1,
    mlp_b1,
    mlp_w2,
    mlp_b2,
):
    link_rows = link_in[0]
    feat_width = link_rows.shape[1]
    link_count = link_rows.shape[0]
    serve_rows = serve_index[0, :, 0, :]
    group_size, slot_cap = serve_rows.shape
    serve_flat = serve_rows.reshape(-1)
    slot_ids = hop_slots[0].T
    hop_count, flow_count = slot_ids.shape
    flat_slots = slot_ids.reshape(-1)
    live_mask = (jnp.arange(hop_count, dtype=jnp.int32)[:, None] < hop_lens[0][None, :]).astype(
        jnp.float32
    )
    fetched = swap_slots(jnp.take(link_rows, serve_rows, axis=0))
    hop_inputs = jnp.take(fetched.reshape(group_size * slot_cap, feat_width), slot_ids, axis=0)
    states = gru_forward(path_in[0], hop_inputs, live_mask, gru_wx, gru_wh, gru_bias)[0]
    partial_value = jax.ops.segment_sum(
        (states * live_mask[:, :, None]).reshape(hop_count * flow_count, feat_width),
        flat_slots,
        num_segments=group_size * slot_cap,
    ).astype(jnp.bfloat16)
    arrived = swap_slots(partial_value.reshape(group_size, slot_cap, feat_width))
    aggregate = jax.ops.segment_sum(
        arrived.reshape(group_size * slot_cap, feat_width).astype(jnp.float32),
        serve_flat,
        num_segments=link_count,
    )
    agg_bf = aggregate.astype(jnp.bfloat16)
    keep_col = (1 - failed[0]).astype(jnp.float32)[:, None]
    link_out, pre_act, activ = link_forward(
        link_rows, agg_bf, keep_col, mlp_w1, mlp_b1, mlp_w2, mlp_b2
    )
    path_out = states[-1].astype(jnp.bfloat16)
    link_direct, agg_grad, mlp_terms = link_backward(
        link_grad[0], link_rows, agg_bf, keep_col, pre_act, activ, mlp_w1, mlp_w2
    )
    returned = swap_slots(jnp.take(agg_grad, serve_rows, axis=0))
    hop_grads = (
        jnp.take(returned.reshape(group_size * slot_cap, feat_width), slot_ids, axis=0).astype(
            jnp.float32
        )
        * live_mask[:, :, None]
    )
    finished, grad_inputs = gru_backward(
        path_in[0], states, hop_inputs, live_mask, hop_grads, path_grad[0], gru_wx, gru_wh, gru_bias
    )
    dpart = jax.ops.segment_sum(
        grad_inputs.reshape(hop_count * flow_count, feat_width),
        flat_slots,
        num_segments=group_size * slot_cap,
    ).astype(jnp.bfloat16)
    owned = swap_slots(dpart.reshape(group_size, slot_cap, feat_width))
    link_back = link_direct + jax.ops.segment_sum(
        owned.reshape(group_size * slot_cap, feat_width).astype(jnp.float32),
        serve_flat,
        num_segments=link_count,
    )
    summed = lax.psum(
        (
            finished[1],
            finished[2],
            finished[3],
            mlp_terms[0],
            mlp_terms[1],
            mlp_terms[2],
            mlp_terms[3],
        ),
        ("replica", "outer", "link"),
    )
    device_count = lax.axis_size("replica") * lax.axis_size("outer") * lax.axis_size("link")
    grad_scale = float(device_count * link_count) ** (-0.5)
    return (
        link_out[None],
        path_out[None],
        link_back[None],
        finished[0][None],
        summed[0] * grad_scale,
        summed[1] * grad_scale,
        summed[2] * grad_scale,
        summed[3] * grad_scale,
        summed[4] * grad_scale,
        summed[5] * grad_scale,
        summed[6] * grad_scale,
    )


def solution(mesh):
    return jax.shard_map(
        body,
        mesh=mesh,
        in_specs=(
            P("replica", ("outer", "link"), None),
            P("replica", ("outer", "link"), None),
            P("replica", ("outer", "link"), None),
            P("replica", ("outer", "link")),
            P("replica", ("outer", "link")),
            P("replica", None, ("outer", "link"), None),
            P("replica", ("outer", "link"), None),
            P("replica", ("outer", "link"), None),
            P(),
            P(),
            P(),
            P(),
            P(),
            P(),
            P(),
        ),
        out_specs=(
            P("replica", ("outer", "link"), None),
            P("replica", ("outer", "link"), None),
            P("replica", ("outer", "link"), None),
            P("replica", ("outer", "link"), None),
            P(),
            P(),
            P(),
            P(),
            P(),
            P(),
            P(),
        ),
        check_vma=False,
    )
```

profile of v0, /device:TPU:2, one launch (start us, length us, event | category | flops | bytes accessed | tf_op | source)
XLA Modules:
  0.0 706.7 jit_solution(12861078215785412026)
XLA Ops:
  8.8 7.6 %gather_fusion = bf16[2048,256]{1,0:T(8,128)(2,1)S(1)} fusion(bf16[512,256]{1,0:T(8,128)(2,1)} %bitcast.135, s32[2048]{0:T(1024)S(1)} %broadcast_clamp_fusion), kind=kCustom, calls=%fused_computation.clone | custom fusion | bytes 2105344 | tf_op jit(solution)/shard_map/jit(_take)/gather | solution.py:187
  17.7 11.5 %all-to-all-start = ((bf16[32,64,256]{2,1,0:T(8,128)(2,1)}), bf16[32,64,256]{2,1,0:T(8,128)(2,1)S(1)}, u32[]{:S(2)}, u32[]{:S(2)}) async-start(bf16[32,64,256]{2,1,0:T(8,128)(2,1)} %broadcast_select_fusion.2), calls=%async_computation | async-start | bytes 2097152 | tf_op jit(solution)/shard_map/all_to_all | solution.py:155
  29.9 27.9 %all-to-all-done = bf16[32,64,256]{2,1,0:T(8,128)(2,1)S(1)} async-done(((bf16[32,64,256]{2,1,0:T(8,128)(2,1)}), bf16[32,64,256]{2,1,0:T(8,128)(2,1)S(1)}, u32[]{:S(2)}, u32[]{:S(2)}) %all-to-all-start) | async-done | bytes 1048608 | tf_op jit(solution)/shard_map/all_to_all | solution.py:155
  57.8 13.0 %gather_fusion.1 = bf16[3072,256]{1,0:T(8,128)(2,1)} fusion(bf16[2048,256]{1,0:T(8,128)(2,1)S(1)} %bitcast.137, s32[3072]{0:T(1024)S(1)} %bitcast_clamp_fusion), kind=kCustom, calls=%fused_computation.1.clone | custom fusion | bytes 3158016 | tf_op jit(solution)/shard_map/jit(_take)/gather | solution.py:188
  70.7 1.7 broadcast_select_fusion
  72.5 2.0 broadcast.84.clone
  74.6 29.4 %while.35 = (s32[]{:T(128)}, f32[128,256]{1,0:T(8,128)S(1)}, f32[24,128,256]{2,1,0:T(8,128)}, f32[24,128]{1,0:T(8,128)S(1)}, bf16[24,128,256]{2,1,0:T(8,128)(2,1...) while((s32[]{:T(128)}, f32[128,256]{1,0:T(8,128)S(1)}, ...), condition=%wide.region_1.4_spmd, body=%wide.region_0.3_spmd.sunk | while | flops 101253248 | bytes 2954097 | solution.py:36
  104.0 4.6 broadcast_multiply_fusion
  108.5 17.9 %scatter_custom_fusion = f32[2048,256]{1,0:T(8,128)S(1)} fusion(s32[3072]{0:T(1024)S(1)} %bitcast.155, f32[3072,256]{1,0:T(8,128)} %bitcast.148, f32[]{:T(128)} %constant.108.clone.1), kind=kCustom, calls=%fused_computation.102 | custom fusion | flops 786432 | bytes 2097664 | tf_op jit(solution)/shard_map/scatter-add | solution.py:190
  127.6 5.2 all-to-all-start.1
  135.5 25.6 %all-to-all-done.1 = bf16[32,64,256]{2,1,0:T(8,128)(2,1)S(1)} async-done(((bf16[32,64,256]{2,1,0:T(8,128)(2,1)}), bf16[32,64,256]{2,1,0:T(8,128)(2,1)S(1)}, u32[]{:S(2)}, u32[]{:S(2)}) %all-to-all-start.1) | async-done | bytes 1048608 | tf_op jit(solution)/shard_map/all_to_all | solution.py:155
  161.1 11.9 %scatter_custom_fusion.1 = f32[512,256]{1,0:T(8,128)S(1)} fusion(s32[2048]{0:T(1024)} %reshape.174, bf16[2048,256]{1,0:T(8,128)(2,1)S(1)} %bitcast.146, f32[]{:T(128)} %constant.108.clone.1), kind=kCustom, calls=%fused_computation.84 | custom fusion | flops 1048576 | bytes 1573376 | tf_op jit(solution)/shard_map/scatter-add | solution.py:196
  173.9 2.1 fusion.85
  177.0 7.5 %gather_fusion.2 = bf16[2048,256]{1,0:T(8,128)(2,1)S(1)} fusion(bf16[512,256]{1,0:T(8,128)(2,1)S(1)} %convolution_convert_fusion, s32[2048]{0:T(1024)S(1)} %broadcast_clamp_fusion), kind=kCustom, calls=%fused_computation.2.clone | custom fusion | bytes 2105344 | tf_op jit(solution)/shard_map/jit(_take)/gather | solution.py:210
  185.7 4.9 all-to-all-start.2
  192.7 1.5 bitcast_convert_fusion.3
  194.2 2.1 slice.91
  196.4 1.8 pad_maximum_fusion.1
  200.7 18.2 %all-to-all-done.2 = bf16[32,64,256]{2,1,0:T(8,128)(2,1)S(1)} async-done(((bf16[32,64,256]{2,1,0:T(8,128)(2,1)}), bf16[32,64,256]{2,1,0:T(8,128)(2,1)S(1)}, u32[]{:S(2)}, u32[]{:S(2)}) %all-to-all-start.2) | async-done | bytes 1048608 | tf_op jit(solution)/shard_map/all_to_all | solution.py:155
  218.9 12.9 %gather_fusion.3 = bf16[3072,256]{1,0:T(8,128)(2,1)} fusion(bf16[2048,256]{1,0:T(8,128)(2,1)S(1)} %bitcast.136, s32[3072]{0:T(1024)S(1)} %copy-done.32), kind=kCustom, calls=%fused_computation.3.clone | custom fusion | bytes 3158016 | tf_op jit(solution)/shard_map/jit(_take)/gather | solution.py:212
  231.9 4.1 convert_multiply_fusion
  236.0 2.1 broadcast.84
  238.1 176.1 %while.36 = (s32[]{:T(128)}, f32[128,256]{1,0:T(8,128)S(1)}, f32[256,768]{1,0:T(8,128)S(1)}, f32[256,768]{1,0:T(8,128)S(1)}, f32[768]{0:T(1024)S(1)}, /*index=5*...) while((s32[]{:T(128)}, f32[128,256]{1,0:T(8,128)S(1)}, ...), condition=%wide.region_6.9_spmd.clone, body=%wide.region_4.8_spmd.clone.sunk | while | flops 306152320 | bytes 12996093 | solution.py:108
  242.0 1.3 convolution_add_fusion.15
  249.3 1.3 convolution_add_fusion.15
  256.7 1.3 convolution_add_fusion.15
  264.0 1.3 convolution_add_fusion.15
  271.3 1.3 convolution_add_fusion.15
  278.6 1.3 convolution_add_fusion.15
  286.0 1.3 convolution_add_fusion.15
  293.3 1.3 convolution_add_fusion.15
  300.7 1.3 convolution_add_fusion.15
  308.0 1.3 convolution_add_fusion.15
  315.3 1.3 convolution_add_fusion.15
  352.0 1.3 convolution_add_fusion.15
  366.7 1.3 convolution_add_fusion.15
  381.4 1.3 convolution_add_fusion.15
  388.7 1.3 convolution_add_fusion.15
  396.0 1.3 convolution_add_fusion.15
  403.4 1.3 convolution_add_fusion.15
  415.5 1.5 slice.215
  417.0 17.9 %scatter_custom_fusion.2 = f32[2048,256]{1,0:T(8,128)S(1)} fusion(s32[3072]{0:T(1024)} %bitcast.154, f32[3072,256]{1,0:T(8,128)} %bitcast.147, f32[]{:T(128)} %constant.108.clone.1), kind=kCustom, calls=%fused_computation.100 | custom fusion | flops 786432 | bytes 2097664 | tf_op jit(solution)/shard_map/scatter-add | solution.py:220
  436.0 5.1 all-to-all-start.3
  442.4 76.8 %all-reduce = (f32[768]{0:T(1024)S(1)}, f32[256]{0:T(256)S(1)}, f32[256]{0:T(256)S(1)}) all-reduce(f32[768]{0:T(1024)S(1)} %get-tuple-element.357, f32[256]{0:T(256)S(1)} %copy-done.39, f32[256]{0:T(256)S(1)} %fusion.64), channel_id=1, replica_groups=mesh['replica'=8,'outer'=4,'link'=8] {'replica','outer','link'}, use_global_device_ids=true, to_apply=%region_11.14 | all-reduce | flops 1280 | bytes 10240 | tf_op jit(solution)/shard_map/psum | solution.py:231
  520.9 160.5 %all-reduce.4.cloned.1.call-done = (f32[256,768]{1,0:T(8,128)}, f32[256,768]{1,0:T(8,128)}, f32[512,256]{1,0:T(8,128)}, f32[256,256]{1,0:T(8,128)}) async-done(((f32[256,768]{1,0:T(8,128)}, f32[256,768]{1,0:T(8,128)}, f32[512,256]{1,0:T(8,128)}, f32[256,256]{1,0:T(8,128)}), (f32[256,768]{1,0:T(8,128)}, f32[256,768]{1,0:T(8,128)}, f32[512,256]{1,0:T(8,128)}, ...) | async-done | bytes 2359312 | tf_op jit(solution)/shard_map/psum | solution.py:231
  681.5 1.8 broadcast_multiply_fusion.4
  683.3 1.9 broadcast_multiply_fusion.3
  687.1 12.0 %scatter_custom_fusion.3 = f32[512,256]{1,0:T(8,128)S(1)} fusion(f32[512,256]{1,0:T(8,128)S(1)} %convolution_add_fusion.5, s32[2048]{0:T(1024)} %reshape.174, bf16[2048,256]{1,0:T(8,128)(2,1)S(1)} %bitcast.145), kind=kCustom, calls=%fused_computation.82 | custom fusion | flops 1048576 | bytes 1572864 | tf_op jit(solution)/shard_map/scatter-add | solution.py:226
  (535 shorter events, 204.2 us)
Async XLA Ops:
  7.2 166.7 %copy-start = (bf16[256,256]{1,0:T(8,128)(2,1)S(1)}, bf16[256,256]{1,0:T(8,128)(2,1)}, u32[]{:S(2)}) copy-start(bf16[256,256]{1,0:T(8,128)(2,1)} %param.36) | copy-start | bytes 393220
  16.4 12.8 %copy-start.34 = (s32[1,128,24]{1,2,0:T(8,128)S(1)}, s32[1,128,24]{1,2,0:T(8,128)}, u32[]{:S(2)}) copy-start(s32[1,128,24]{1,2,0:T(8,128)} %param.25) | copy-start | bytes 36868
  16.4 12.8 %copy-start.40 = (s32[1,128]{1,0:T(1,128)S(1)}, s32[1,128]{1,0:T(1,128)}, u32[]{:S(2)}) copy-start(s32[1,128]{1,0:T(1,128)} %param.26) | copy-start | bytes 1540
  16.4 12.8 %copy-start.33 = (bf16[1,128,256]{2,1,0:T(8,128)(2,1)S(1)}, bf16[1,128,256]{2,1,0:T(8,128)(2,1)}, u32[]{:S(2)}) copy-start(bf16[1,128,256]{2,1,0:T(8,128)(2,1)} %param.24) | copy-start | bytes 196612
  17.7 40.1 %all-to-all-start = ((bf16[32,64,256]{2,1,0:T(8,128)(2,1)}), bf16[32,64,256]{2,1,0:T(8,128)(2,1)S(1)}, u32[]{:S(2)}, u32[]{:S(2)}) async-start(bf16[32,64,256]{2,1,0:T(8,128)(2,1)} %broadcast_select_fusion.2), calls=%async_computation | async-start | bytes 2097152 | tf_op jit(solution)/shard_map/all_to_all | solution.py:155
  29.2 41.6 %copy-start.31 = (s32[3072]{0:T(1024)}, s32[3072]{0:T(1024)S(1)}, u32[]{:S(2)}) copy-start(s32[3072]{0:T(1024)S(1)} %bitcast_clamp_fusion) | copy-start | bytes 36868
  29.2 41.5 %copy-start.35 = (pred[24,128]{1,0:T(8,128)(4,1)}, pred[24,128]{1,0:T(8,128)(4,1)S(1)}, u32[]{:S(2)}) copy-start(pred[24,128]{1,0:T(8,128)(4,1)S(1)} %get-tuple-element.474) | copy-start | bytes 9220
  104.0 4.6 copy-start.12
  104.0 4.6 copy-start.29
  126.5 8.8 %copy-start.1 = (bf16[1,512,256]{2,1,0:T(8,128)(2,1)S(1)}, bf16[1,512,256]{2,1,0:T(8,128)(2,1)}, u32[]{:S(2)}) copy-start(bf16[1,512,256]{2,1,0:T(8,128)(2,1)} %param.23) | copy-start | bytes 786436
  126.5 8.8 %copy-start.13 = (bf16[512,256]{1,0:T(8,128)(2,1)S(1)}, bf16[512,256]{1,0:T(8,128)(2,1)}, u32[]{:S(2)}) copy-start(bf16[512,256]{1,0:T(8,128)(2,1)} %param.34) | copy-start | bytes 786436
  127.6 5.8 copy-start.28
  127.6 7.1 %copy-start.38 = (s32[1,512]{1,0:T(1,128)S(1)}, s32[1,512]{1,0:T(1,128)}, u32[]{:S(2)}) copy-start(s32[1,512]{1,0:T(1,128)} %param.27) | copy-start | bytes 6148
  127.6 45.4 %copy-start.14 = (bf16[512,256]{1,0:T(8,128)(2,1)S(1)}, bf16[512,256]{1,0:T(8,128)(2,1)}, u32[]{:S(2)}) copy-start(bf16[512,256]{1,0:T(8,128)(2,1)} %param.34) | copy-start | bytes 786436
  127.6 33.5 %all-to-all-start.1 = ((bf16[32,64,256]{2,1,0:T(8,128)(2,1)}), bf16[32,64,256]{2,1,0:T(8,128)(2,1)S(1)}, u32[]{:S(2)}, u32[]{:S(2)}) async-start(bf16[32,64,256]{2,1,0:T(8,128)(2,1)} %bitcast.142), calls=%async_computation.1 | async-start | bytes 2097152 | tf_op jit(solution)/shard_map/all_to_all | solution.py:155
  185.7 33.2 %all-to-all-start.2 = ((bf16[32,64,256]{2,1,0:T(8,128)(2,1)}), bf16[32,64,256]{2,1,0:T(8,128)(2,1)S(1)}, u32[]{:S(2)}, u32[]{:S(2)}) async-start(bf16[32,64,256]{2,1,0:T(8,128)(2,1)} %broadcast_select_fusion.1), calls=%async_computation.2 | async-start | bytes 2097152 | tf_op jit(solution)/shard_map/all_to_all | solution.py:155
  190.6 490.8 %all-reduce.4.cloned.1.call-start = ((), (), s32[]{:S(2)}) async-start(), calls=%async_computation.4 | async-start | bytes 4718592 | tf_op jit(solution)/shard_map/psum | solution.py:231
  198.8 20.2 %copy-start.32 = (s32[3072]{0:T(1024)S(1)}, s32[3072]{0:T(1024)}, u32[]{:S(2)}) copy-start(s32[3072]{0:T(1024)} %copy-done.31) | copy-start | bytes 36868
  218.9 12.9 %copy-start.30 = (f32[24,128]{1,0:T(8,128)S(1)}, f32[24,128]{1,0:T(8,128)}, u32[]{:S(2)}) copy-start(f32[24,128]{1,0:T(8,128)} %copy-done.29) | copy-start | bytes 36868
  218.9 13.0 %copy-start.36 = (pred[24,128]{1,0:T(8,128)(4,1)S(1)}, pred[24,128]{1,0:T(8,128)(4,1)}, u32[]{:S(2)}) copy-start(pred[24,128]{1,0:T(8,128)(4,1)} %copy-done.35) | copy-start | bytes 9220
  239.2 2.4 copy-start.27
  246.6 2.4 copy-start.27
  253.9 2.4 copy-start.27
  268.6 2.4 copy-start.27
  283.2 2.4 copy-start.27
  290.6 2.4 copy-start.27
  297.9 2.4 copy-start.27
  312.6 2.4 copy-start.27
  319.9 2.4 copy-start.27
  334.6 2.4 copy-start.27
  341.9 2.4 copy-start.27
  349.3 2.4 copy-start.27
  356.6 2.4 copy-start.27
  363.9 2.4 copy-start.27
  371.3 2.4 copy-start.27
  378.6 2.4 copy-start.27
  385.9 2.4 copy-start.27
  393.3 2.4 copy-start.27
  400.6 2.4 copy-start.27
  407.9 2.4 copy-start.27
  414.1 20.8 %copy-start.8 = (f32[128,256]{1,0:T(8,128)}, f32[128,256]{1,0:T(8,128)S(1)}, u32[]{:S(2)}) copy-start(f32[128,256]{1,0:T(8,128)S(1)} %get-tuple-element.354) | copy-start | bytes 393220
  434.9 6.2 copy-start.41
  436.0 5.1 copy-start.22
  436.0 6.1 copy-start.11
  436.0 6.1 copy-start.15
  436.0 251.0 %all-to-all-start.3 = ((bf16[32,64,256]{2,1,0:T(8,128)(2,1)}), bf16[32,64,256]{2,1,0:T(8,128)(2,1)S(1)}, u32[]{:S(2)}, u32[]{:S(2)}) async-start(bf16[32,64,256]{2,1,0:T(8,128)(2,1)} %bitcast.141), calls=%async_computation.3 | async-start | bytes 2097152 | tf_op jit(solution)/shard_map/all_to_all | solution.py:155
  681.5 3.7 copy-start.19
  681.5 4.6 copy-start.18
  (22 other events, 38.1 us)
Sparse Core Ops, SparseCore 0:
  415.4 265.9 all-reduce.3
where the time goes:
time: 711 us; the launch traced here: 707 us
  waiting for transfers between devices  232 us (33%)
  matrix products  158 us (22%)
  other arithmetic  141 us (20%)
  blocking collectives  76.8 us (11%)
  local copies, waits for them, and re-layouts  54.8 us (8%)
  starting transfers between devices  26.9 us (4%)
  between operations  14.5 us (2%)
    psum x1, waiting for transfers between devices, body(): lax.psum((finished[1], finished[2], finished[3], mlp_terms[0], mlp_terms[...  161 us
    psum x1, blocking collectives, body(): lax.psum((finished[1], finished[2], finished[3], mlp_terms[0], mlp_terms[...  76.8 us
    all_to_all x4, waiting for transfers between devices, swap_slots(): lax.all_to_all(blocks, ('outer', 'link'), split_axis=0, concat_axis=0, ti...  71.6 us
    dot_general x48, matrix products, gate_terms(): jnp.dot(hop_input, input_weight, preferred_element_type=jnp.float32)  31.8 us
    dot_general x48, matrix products, gate_terms(): jnp.dot(state_now.astype(jnp.bfloat16), hidden_weight, preferred_element_...  31.7 us
    dot_general x24, matrix products, back_step(): jnp.dot(state_now.astype(jnp.bfloat16).T, hid_bf, preferred_element_type=...  31 us
    dot_general x24, matrix products, back_step(): jnp.dot(hop_input.T, in_bf, preferred_element_type=jnp.float32)  29.4 us
    all_to_all x4, starting transfers between devices, swap_slots(): lax.all_to_all(blocks, ('outer', 'link'), split_axis=0, concat_axis=0, ti...  26.7 us
  transfers between devices with their start and end apart: 5, of which 4 were waited for; matrix products, arithmetic and copies ran while one was open for 6% of the time, Pallas kernels for 0%

commit v1 on v0

--- a/solution.py
+++ b/solution.py
@@ -229,16 +229,19 @@
         num_segments=link_count,
     )
     summed = lax.psum(
-        (
-            finished[1],
-            finished[2],
-            finished[3],
-            mlp_terms[0],
-            mlp_terms[1],
-            mlp_terms[2],
-            mlp_terms[3],
+        lax.psum(
+            (
+                finished[1],
+                finished[2],
+                finished[3],
+                mlp_terms[0],
+                mlp_terms[1],
+                mlp_terms[2],
+                mlp_terms[3],
+            ),
+            "replica",
         ),
-        ("replica", "outer", "link"),
+        ("outer", "link"),
     )
     device_count = lax.axis_size("replica") * lax.axis_size("outer") * lax.axis_size("link")
     grad_scale = float(device_count * link_count) ** (-0.5)

time: 711 us -> 675 us (0.949)
  waiting for transfers between devices: 232 us -> 174 us
  blocking collectives: 76.8 us -> 95.8 us
    psum x1, waiting for transfers between devices: 161 us -> 65.9 us  [body(): lax.psum((finished[1], finished[2], finished[3], mlp_terms[0], mlp_terms[...]
    psum x0 -> x1, blocking collectives: none -> 82.1 us  [body(): lax.psum(lax.psum((finished[1], finished[2], finished[3], mlp_terms[0], m...]
    psum x1, blocking collectives: 76.8 us -> 13.7 us  [body(): lax.psum((finished[1], finished[2], finished[3], mlp_terms[0], mlp_terms[...]
    psum x0 -> x1, waiting for transfers between devices: none -> 36.1 us  [body(): lax.psum(lax.psum((finished[1], finished[2], finished[3], mlp_terms[0], m...]
  transfers between devices with their start and end apart: 5 -> 6, of which waited for: 4 -> 5; matrix products, arithmetic and copies ran while one was open for 6% -> 7% of each run, Pallas kernels for 0% -> 0%
where the time goes in v1:
time: 675 us; the launch traced here: 671 us
  waiting for transfers between devices  174 us (26%)
  matrix products  158 us (23%)
  other arithmetic  141 us (21%)
  blocking collectives  95.8 us (14%)
  local copies, waits for them, and re-layouts  54 us (8%)
  starting transfers between devices  31.9 us (5%)
  between operations  14.5 us (2%)
    psum x1, blocking collectives, body(): lax.psum(lax.psum((finished[1], finished[2], finished[3], mlp_terms[0], m...  82.1 us
    all_to_all x4, waiting for transfers between devices, swap_slots(): lax.all_to_all(blocks, ('outer', 'link'), split_axis=0, concat_axis=0, ti...  71.7 us
    psum x1, waiting for transfers between devices, body(): lax.psum((finished[1], finished[2], finished[3], mlp_terms[0], mlp_terms[...  65.9 us
    psum x1, waiting for transfers between devices, body(): lax.psum(lax.psum((finished[1], finished[2], finished[3], mlp_terms[0], m...  36.1 us
    dot_general x48, matrix products, gate_terms(): jnp.dot(hop_input, input_weight, preferred_element_type=jnp.float32)  31.8 us
    dot_general x48, matrix products, gate_terms(): jnp.dot(state_now.astype(jnp.bfloat16), hidden_weight, preferred_element_...  31.7 us
    all_to_all x4, starting transfers between devices, swap_slots(): lax.all_to_all(blocks, ('outer', 'link'), split_axis=0, concat_axis=0, ti...  31.6 us
    dot_general x24, matrix products, back_step(): jnp.dot(state_now.astype(jnp.bfloat16).T, hid_bf, preferred_element_type=...  31 us
  transfers between devices with their start and end apart: 6, of which 5 were waited for; matrix products, arithmetic and copies ran while one was open for 7% of the time, Pallas kernels for 0%

profile of v1, /device:TPU:2, one launch (start us, length us, event | category | flops | bytes accessed | tf_op | source)
XLA Modules:
  0.0 671.5 jit_solution(14594991080161460262)
XLA Ops:
  8.8 7.6 %gather_fusion = bf16[2048,256]{1,0:T(8,128)(2,1)S(1)} fusion(bf16[512,256]{1,0:T(8,128)(2,1)} %bitcast.135, s32[2048]{0:T(1024)S(1)} %broadcast_clamp_fusion), kind=kCustom, calls=%fused_computation.clone | custom fusion | bytes 2105344 | tf_op jit(solution)/shard_map/jit(_take)/gather | solution.py:187
  17.7 11.5 %all-to-all-start = ((bf16[32,64,256]{2,1,0:T(8,128)(2,1)}), bf16[32,64,256]{2,1,0:T(8,128)(2,1)S(1)}, u32[]{:S(2)}, u32[]{:S(2)}) async-start(bf16[32,64,256]{2,1,0:T(8,128)(2,1)} %broadcast_select_fusion.2), calls=%async_computation | async-start | bytes 2097152 | tf_op jit(solution)/shard_map/all_to_all | solution.py:155
  29.9 27.9 %all-to-all-done = bf16[32,64,256]{2,1,0:T(8,128)(2,1)S(1)} async-done(((bf16[32,64,256]{2,1,0:T(8,128)(2,1)}), bf16[32,64,256]{2,1,0:T(8,128)(2,1)S(1)}, u32[]{:S(2)}, u32[]{:S(2)}) %all-to-all-start) | async-done | bytes 1048608 | tf_op jit(solution)/shard_map/all_to_all | solution.py:155
  57.8 13.0 %gather_fusion.1 = bf16[3072,256]{1,0:T(8,128)(2,1)} fusion(bf16[2048,256]{1,0:T(8,128)(2,1)S(1)} %bitcast.137, s32[3072]{0:T(1024)S(1)} %bitcast_clamp_fusion), kind=kCustom, calls=%fused_computation.1.clone | custom fusion | bytes 3158016 | tf_op jit(solution)/shard_map/jit(_take)/gather | solution.py:188
  70.7 1.7 broadcast_select_fusion
  72.5 2.0 broadcast.84.clone
  74.6 29.4 %while.35 = (s32[]{:T(128)}, f32[128,256]{1,0:T(8,128)S(1)}, f32[24,128,256]{2,1,0:T(8,128)}, f32[24,128]{1,0:T(8,128)S(1)}, bf16[24,128,256]{2,1,0:T(8,128)(2,1...) while((s32[]{:T(128)}, f32[128,256]{1,0:T(8,128)S(1)}, ...), condition=%wide.region_1.4_spmd, body=%wide.region_0.3_spmd.sunk | while | flops 101253248 | bytes 2954097 | solution.py:36
  104.0 4.6 broadcast_multiply_fusion
  108.5 17.9 %scatter_custom_fusion = f32[2048,256]{1,0:T(8,128)S(1)} fusion(s32[3072]{0:T(1024)S(1)} %bitcast.155, f32[3072,256]{1,0:T(8,128)} %bitcast.148, f32[]{:T(128)} %constant.108.clone.1), kind=kCustom, calls=%fused_computation.102 | custom fusion | flops 786432 | bytes 2097664 | tf_op jit(solution)/shard_map/scatter-add | solution.py:190
  127.6 5.2 all-to-all-start.1
  135.5 25.6 %all-to-all-done.1 = bf16[32,64,256]{2,1,0:T(8,128)(2,1)S(1)} async-done(((bf16[32,64,256]{2,1,0:T(8,128)(2,1)}), bf16[32,64,256]{2,1,0:T(8,128)(2,1)S(1)}, u32[]{:S(2)}, u32[]{:S(2)}) %all-to-all-start.1) | async-done | bytes 1048608 | tf_op jit(solution)/shard_map/all_to_all | solution.py:155
  161.1 11.9 %scatter_custom_fusion.1 = f32[512,256]{1,0:T(8,128)S(1)} fusion(s32[2048]{0:T(1024)} %reshape.174, bf16[2048,256]{1,0:T(8,128)(2,1)S(1)} %bitcast.146, f32[]{:T(128)} %constant.108.clone.1), kind=kCustom, calls=%fused_computation.84 | custom fusion | flops 1048576 | bytes 1573376 | tf_op jit(solution)/shard_map/scatter-add | solution.py:196
  173.9 2.1 fusion.85
  177.0 7.5 %gather_fusion.2 = bf16[2048,256]{1,0:T(8,128)(2,1)S(1)} fusion(bf16[512,256]{1,0:T(8,128)(2,1)S(1)} %convolution_convert_fusion, s32[2048]{0:T(1024)S(1)} %broadcast_clamp_fusion), kind=kCustom, calls=%fused_computation.2.clone | custom fusion | bytes 2105344 | tf_op jit(solution)/shard_map/jit(_take)/gather | solution.py:210
  185.7 4.9 all-to-all-start.2
  192.7 1.5 bitcast_convert_fusion.3
  194.2 2.1 slice.91
  196.3 1.8 pad_maximum_fusion.1
  200.7 18.2 %all-to-all-done.2 = bf16[32,64,256]{2,1,0:T(8,128)(2,1)S(1)} async-done(((bf16[32,64,256]{2,1,0:T(8,128)(2,1)}), bf16[32,64,256]{2,1,0:T(8,128)(2,1)S(1)}, u32[]{:S(2)}, u32[]{:S(2)}) %all-to-all-start.2) | async-done | bytes 1048608 | tf_op jit(solution)/shard_map/all_to_all | solution.py:155
  218.9 12.9 %gather_fusion.3 = bf16[3072,256]{1,0:T(8,128)(2,1)} fusion(bf16[2048,256]{1,0:T(8,128)(2,1)S(1)} %bitcast.136, s32[3072]{0:T(1024)S(1)} %copy-done.32), kind=kCustom, calls=%fused_computation.3.clone | custom fusion | bytes 3158016 | tf_op jit(solution)/shard_map/jit(_take)/gather | solution.py:212
  231.9 4.1 convert_multiply_fusion
  236.0 2.1 broadcast.84
  238.1 176.1 %while.36 = (s32[]{:T(128)}, f32[128,256]{1,0:T(8,128)S(1)}, f32[256,768]{1,0:T(8,128)S(1)}, f32[256,768]{1,0:T(8,128)S(1)}, f32[768]{0:T(1024)S(1)}, /*index=5*...) while((s32[]{:T(128)}, f32[128,256]{1,0:T(8,128)S(1)}, ...), condition=%wide.region_6.9_spmd.clone, body=%wide.region_4.8_spmd.clone.sunk | while | flops 306152320 | bytes 12996093 | solution.py:108
  242.0 1.3 convolution_add_fusion.15
  249.3 1.3 convolution_add_fusion.15
  256.7 1.3 convolution_add_fusion.15
  264.0 1.3 convolution_add_fusion.15
  271.3 1.3 convolution_add_fusion.15
  286.0 1.3 convolution_add_fusion.15
  293.3 1.3 convolution_add_fusion.15
  300.7 1.3 convolution_add_fusion.15
  315.3 1.3 convolution_add_fusion.15
  352.0 1.3 convolution_add_fusion.15
  366.7 1.3 convolution_add_fusion.15
  381.4 1.3 convolution_add_fusion.15
  388.7 1.3 convolution_add_fusion.15
  396.0 1.3 convolution_add_fusion.15
  403.4 1.3 convolution_add_fusion.15
  415.4 65.9 %all-reduce.9.cloned.1.call-done = (f32[256,768]{1,0:T(8,128)}, f32[256,768]{1,0:T(8,128)}, f32[512,256]{1,0:T(8,128)}, f32[256,256]{1,0:T(8,128)}) async-done(((f32[256,768]{1,0:T(8,128)}, f32[256,768]{1,0:T(8,128)}, f32[512,256]{1,0:T(8,128)}, f32[256,256]{1,0:T(8,128)}), (f32[256,768]{1,0:T(8,128)}, f32[256,768]{1,0:T(8,128)}, f32[512,256]{1,0:T(8,128)}, ...) | async-done | bytes 2359312 | tf_op jit(solution)/shard_map/psum | solution.py:232
  481.3 17.9 %scatter_custom_fusion.2 = f32[2048,256]{1,0:T(8,128)S(1)} fusion(s32[3072]{0:T(1024)} %bitcast.154, f32[3072,256]{1,0:T(8,128)} %bitcast.147, f32[]{:T(128)} %constant.108.clone.1), kind=kCustom, calls=%fused_computation.100 | custom fusion | flops 786432 | bytes 2097664 | tf_op jit(solution)/shard_map/scatter-add | solution.py:220
  500.3 10.0 %all-to-all-start.3 = ((bf16[32,64,256]{2,1,0:T(8,128)(2,1)}), bf16[32,64,256]{2,1,0:T(8,128)(2,1)S(1)}, u32[]{:S(2)}, u32[]{:S(2)}) async-start(bf16[32,64,256]{2,1,0:T(8,128)(2,1)} %bitcast.141), calls=%async_computation.3 | async-start | bytes 2097152 | tf_op jit(solution)/shard_map/all_to_all | solution.py:155
  510.5 1.5 slice.215
  513.3 13.7 %all-reduce.2 = (f32[768]{0:T(1024)S(1)}, f32[256]{0:T(256)S(1)}, f32[256]{0:T(256)S(1)}) all-reduce(f32[768]{0:T(1024)S(1)} %get-tuple-element.357, f32[256]{0:T(256)S(1)} %copy-done.39, f32[256]{0:T(256)S(1)} %fusion.64), channel_id=1, replica_groups=mesh['replica'=8,'outer'=4,'link'=8] {'replica'}, use_global_device_ids=true, to_apply=%region_13.16 | all-reduce | flops 1280 | bytes 10240 | tf_op jit(solution)/shard_map/psum | solution.py:232
  527.0 82.1 %all-reduce = (f32[768]{0:T(1024)S(1)}, f32[256]{0:T(256)S(1)}, f32[256]{0:T(256)S(1)}) all-reduce(f32[768]{0:T(1024)S(1)} %get-tuple-element.459, f32[256]{0:T(256)S(1)} %get-tuple-element.460, f32[256]{0:T(256)S(1)} %get-tuple-element.461), channel_id=1, replica_groups=mesh['replica'=8,'outer'=4,'link'=8] {'outer','link'}, use_global_device_ids=true, to_apply=%region_14.17 | all-reduce | flops 1280 | bytes 10240 | tf_op jit(solution)/shard_map/psum | solution.py:231
  610.9 12.0 %scatter_custom_fusion.3 = f32[512,256]{1,0:T(8,128)S(1)} fusion(f32[512,256]{1,0:T(8,128)S(1)} %convolution_add_fusion.5, s32[2048]{0:T(1024)} %reshape.174, bf16[2048,256]{1,0:T(8,128)(2,1)S(1)} %bitcast.145), kind=kCustom, calls=%fused_computation.82 | custom fusion | flops 1048576 | bytes 1572864 | tf_op jit(solution)/shard_map/scatter-add | solution.py:226
  622.8 36.1 %all-reduce.7.cloned.1.call-done = (f32[256,768]{1,0:T(8,128)}, f32[256,768]{1,0:T(8,128)}, f32[512,256]{1,0:T(8,128)}, f32[256,256]{1,0:T(8,128)}) async-done(((f32[256,768]{1,0:T(8,128)}, f32[256,768]{1,0:T(8,128)}, f32[512,256]{1,0:T(8,128)}, f32[256,256]{1,0:T(8,128)}), (f32[256,768]{1,0:T(8,128)}, f32[256,768]{1,0:T(8,128)}, f32[512,256]{1,0:T(8,128)}, ...) | async-done | bytes 2359312 | tf_op jit(solution)/shard_map/psum | solution.py:231
  659.0 2.2 broadcast_multiply_fusion.2
  661.2 1.7 broadcast_multiply_fusion.4
  (539 shorter events, 205.9 us)
Async XLA Ops:
  7.2 166.7 %copy-start = (bf16[256,256]{1,0:T(8,128)(2,1)S(1)}, bf16[256,256]{1,0:T(8,128)(2,1)}, u32[]{:S(2)}) copy-start(bf16[256,256]{1,0:T(8,128)(2,1)} %param.36) | copy-start | bytes 393220
  16.4 12.8 %copy-start.34 = (s32[1,128,24]{1,2,0:T(8,128)S(1)}, s32[1,128,24]{1,2,0:T(8,128)}, u32[]{:S(2)}) copy-start(s32[1,128,24]{1,2,0:T(8,128)} %param.25) | copy-start | bytes 36868
  16.4 12.8 %copy-start.40 = (s32[1,128]{1,0:T(1,128)S(1)}, s32[1,128]{1,0:T(1,128)}, u32[]{:S(2)}) copy-start(s32[1,128]{1,0:T(1,128)} %param.26) | copy-start | bytes 1540
  16.4 12.8 %copy-start.33 = (bf16[1,128,256]{2,1,0:T(8,128)(2,1)S(1)}, bf16[1,128,256]{2,1,0:T(8,128)(2,1)}, u32[]{:S(2)}) copy-start(bf16[1,128,256]{2,1,0:T(8,128)(2,1)} %param.24) | copy-start | bytes 196612
  17.7 40.1 %all-to-all-start = ((bf16[32,64,256]{2,1,0:T(8,128)(2,1)}), bf16[32,64,256]{2,1,0:T(8,128)(2,1)S(1)}, u32[]{:S(2)}, u32[]{:S(2)}) async-start(bf16[32,64,256]{2,1,0:T(8,128)(2,1)} %broadcast_select_fusion.2), calls=%async_computation | async-start | bytes 2097152 | tf_op jit(solution)/shard_map/all_to_all | solution.py:155
  29.2 41.6 %copy-start.31 = (s32[3072]{0:T(1024)}, s32[3072]{0:T(1024)S(1)}, u32[]{:S(2)}) copy-start(s32[3072]{0:T(1024)S(1)} %bitcast_clamp_fusion) | copy-start | bytes 36868
  29.2 41.5 %copy-start.35 = (pred[24,128]{1,0:T(8,128)(4,1)}, pred[24,128]{1,0:T(8,128)(4,1)S(1)}, u32[]{:S(2)}) copy-start(pred[24,128]{1,0:T(8,128)(4,1)S(1)} %get-tuple-element.481) | copy-start | bytes 9220
  104.0 4.6 copy-start.12
  104.0 4.6 copy-start.29
  126.5 8.8 %copy-start.1 = (bf16[1,512,256]{2,1,0:T(8,128)(2,1)S(1)}, bf16[1,512,256]{2,1,0:T(8,128)(2,1)}, u32[]{:S(2)}) copy-start(bf16[1,512,256]{2,1,0:T(8,128)(2,1)} %param.23) | copy-start | bytes 786436
  126.5 8.8 %copy-start.13 = (bf16[512,256]{1,0:T(8,128)(2,1)S(1)}, bf16[512,256]{1,0:T(8,128)(2,1)}, u32[]{:S(2)}) copy-start(bf16[512,256]{1,0:T(8,128)(2,1)} %param.34) | copy-start | bytes 786436
  127.6 5.8 copy-start.28
  127.6 7.1 %copy-start.38 = (s32[1,512]{1,0:T(1,128)S(1)}, s32[1,512]{1,0:T(1,128)}, u32[]{:S(2)}) copy-start(s32[1,512]{1,0:T(1,128)} %param.27) | copy-start | bytes 6148
  127.6 45.4 %copy-start.14 = (bf16[512,256]{1,0:T(8,128)(2,1)S(1)}, bf16[512,256]{1,0:T(8,128)(2,1)}, u32[]{:S(2)}) copy-start(bf16[512,256]{1,0:T(8,128)(2,1)} %param.34) | copy-start | bytes 786436
  127.6 33.5 %all-to-all-start.1 = ((bf16[32,64,256]{2,1,0:T(8,128)(2,1)}), bf16[32,64,256]{2,1,0:T(8,128)(2,1)S(1)}, u32[]{:S(2)}, u32[]{:S(2)}) async-start(bf16[32,64,256]{2,1,0:T(8,128)(2,1)} %bitcast.142), calls=%async_computation.1 | async-start | bytes 2097152 | tf_op jit(solution)/shard_map/all_to_all | solution.py:155
  185.7 33.2 %all-to-all-start.2 = ((bf16[32,64,256]{2,1,0:T(8,128)(2,1)}), bf16[32,64,256]{2,1,0:T(8,128)(2,1)S(1)}, u32[]{:S(2)}, u32[]{:S(2)}) async-start(bf16[32,64,256]{2,1,0:T(8,128)(2,1)} %broadcast_select_fusion.1), calls=%async_computation.2 | async-start | bytes 2097152 | tf_op jit(solution)/shard_map/all_to_all | solution.py:155
  190.6 290.6 %all-reduce.9.cloned.1.call-start = ((), (), s32[]{:S(2)}) async-start(), calls=%async_computation.5 | async-start | bytes 4718592 | tf_op jit(solution)/shard_map/psum | solution.py:232
  198.7 20.2 %copy-start.32 = (s32[3072]{0:T(1024)S(1)}, s32[3072]{0:T(1024)}, u32[]{:S(2)}) copy-start(s32[3072]{0:T(1024)} %copy-done.31) | copy-start | bytes 36868
  218.9 12.9 %copy-start.30 = (f32[24,128]{1,0:T(8,128)S(1)}, f32[24,128]{1,0:T(8,128)}, u32[]{:S(2)}) copy-start(f32[24,128]{1,0:T(8,128)} %copy-done.29) | copy-start | bytes 36868
  218.9 13.0 %copy-start.36 = (pred[24,128]{1,0:T(8,128)(4,1)S(1)}, pred[24,128]{1,0:T(8,128)(4,1)}, u32[]{:S(2)}) copy-start(pred[24,128]{1,0:T(8,128)(4,1)} %copy-done.35) | copy-start | bytes 9220
  239.2 2.4 copy-start.27
  246.6 2.4 copy-start.27
  253.9 2.4 copy-start.27
  268.6 2.4 copy-start.27
  283.2 2.4 copy-start.27
  290.6 2.4 copy-start.27
  297.9 2.4 copy-start.27
  312.6 2.4 copy-start.27
  319.9 2.4 copy-start.27
  334.6 2.4 copy-start.27
  341.9 2.4 copy-start.27
  349.3 2.4 copy-start.27
  356.6 2.4 copy-start.27
  363.9 2.4 copy-start.27
  371.3 2.4 copy-start.27
  385.9 2.4 copy-start.27
  407.9 2.4 copy-start.27
  414.1 67.1 %copy-start.8 = (f32[128,256]{1,0:T(8,128)}, f32[128,256]{1,0:T(8,128)S(1)}, u32[]{:S(2)}) copy-start(f32[128,256]{1,0:T(8,128)S(1)} %get-tuple-element.354) | copy-start | bytes 393220
  415.3 243.7 %all-reduce.7.cloned.1.call-start = ((), (), s32[]{:S(2)}) async-start(), calls=%async_computation.4 | async-start | bytes 4718592 | tf_op jit(solution)/shard_map/psum | solution.py:231
  499.2 11.1 %copy-start.17 = (bf16[1,512,256]{2,1,0:T(8,128)(2,1)S(1)}, bf16[1,512,256]{2,1,0:T(8,128)(2,1)}, u32[]{:S(2)}) copy-start(bf16[1,512,256]{2,1,0:T(8,128)(2,1)} %param.29) | copy-start | bytes 786436
  499.2 12.8 %copy-start.41 = (f32[256]{0:T(256)S(1)}, f32[256]{0:T(256)}, u32[]{:S(2)}) copy-start(f32[256]{0:T(256)} %param.37) | copy-start | bytes 3076
  500.3 11.7 %copy-start.21 = (f32[512,256]{1,0:T(8,128)S(1)}, f32[512,256]{1,0:T(8,128)}, u32[]{:S(2)}) copy-start(f32[512,256]{1,0:T(8,128)} %copy-done.19) | copy-start | bytes 1572868
  500.3 110.5 %all-to-all-start.3 = ((bf16[32,64,256]{2,1,0:T(8,128)(2,1)}), bf16[32,64,256]{2,1,0:T(8,128)(2,1)S(1)}, u32[]{:S(2)}, u32[]{:S(2)}) async-start(bf16[32,64,256]{2,1,0:T(8,128)(2,1)} %bitcast.141), calls=%async_computation.3 | async-start | bytes 2097152 | tf_op jit(solution)/shard_map/all_to_all | solution.py:155
  510.3 2.7 copy-start.11
  510.3 2.7 copy-start.15
  622.8 41.8 %copy-start.24 = (f32[512,256]{1,0:T(8,128)}, f32[512,256]{1,0:T(8,128)S(1)}, u32[]{:S(2)}) copy-start(f32[512,256]{1,0:T(8,128)S(1)} %scatter_custom_fusion.3) | copy-start | bytes 1572868
  659.0 3.9 copy-start.23
  659.0 4.7 copy-start.18
  (23 other events, 43.2 us)
Sparse Core Ops, SparseCore 0:
  415.4 65.7 all-reduce.8
  485.2 173.7 all-reduce.6
